TPU v7x, 256 devices: a whole 4x4x8 slice. The times are simulated.
256 devices in a mesh: row: 16 (over x_lo, z), col: 16 (over y, x_hi, core).
Axes of the slice: x: 4 (x_hi: 2, x_lo: 2; x = x_hi * 2 + x_lo), y: 4, z: 8, core: 2. Of those that a mesh axis runs over, the one named last changes fastest.
Arguments:
- features: bfloat16 [1024, 1024, 128], P('row', 'col'), may hold values from -6 to 6
- kernels: bfloat16 [2, 3, 3, 128, 128], replicated, may hold values from -0.1875 to 0.1875
- length: int32 [1], replicated, may hold values from 512 to 1024
- cotangent: bfloat16 [1024, 1024, 128], P('row', 'col'), may hold values from -6 to 6
Outputs:
- output_map: bfloat16 [1024, 1024, 128], P('row', 'col')
- feature_grad: bfloat16 [1024, 1024, 128], P('row', 'col')
- kernel_gradient: float32 [2, 3, 3, 128, 128], replicated
Inputs may be any that keep to these rules, and one draw needn't show every extreme that they name: The protein occupies the first length rows and columns of the pair map.
All inputs are finite; a program needn't handle non-finite values.
Results may differ from a plain program's by a relative error of at most 0.0039.
Values may be sent and summed in bfloat16 or wider, within the bound.
A program may use at most 192 MiB of HBM per device.

v0:
```python
import functools

import jax
import jax.numpy as jnp
from jax import lax
from jax.experimental import pallas as pl
from jax.experimental.pallas import tpu as pltpu
from jax.sharding import PartitionSpec as P

MESH = pl.DeviceIdType.MESH
F32, BF16 = jnp.float32, jnp.bfloat16
FIRST_SPACING = 4
SECOND_SPACING = 8
CELL = 4
ONE, TWO = FIRST_SPACING // CELL, SECOND_SPACING // CELL
T = 16
LANES = 128
SIDES = [(r, c) for r in (-1, 0, 1) for c in (-1, 0, 1) if (r, c) != (0, 0)]
HALF = 72
PIECE = 5
PADDED = 16 * PIECE
WIRE = BF16


def exp_low(values):
    return jnp.exp(jnp.minimum(values, 0.0))


def elu(values):
    return jnp.where(values > 0, values, exp_low(values) - 1.0)


def slope(values):
    return jnp.where(values > 0, 1.0, exp_low(values))


def place():
    i, j = lax.axis_index("row"), lax.axis_index("col")
    x_lo, z = i // 8, i % 8
    y, x_hi, core = j // 4, (j // 2) % 2, j % 2
    return i, j, x_hi * 2 + x_lo, y, z, core


def at(x, y, z, core):
    return ((x % 2) * 8 + z, y * 4 + (x // 2) * 2 + core)


def flip(value, k):
    total = 0
    for bit in (1, 2, 4):
        b = (value // bit) % 2
        total = total + bit * ((1 - b) if k & bit else b)
    return total


def fill_weights(kern, forward, backward, layer):
    zero = jnp.zeros((3 * LANES, LANES), BF16)
    for ref in (forward, backward):
        ref[0 : 3 * LANES, LANES:] = zero
        ref[9 * LANES :, :LANES] = zero
    for p in range(3):
        for q in range(3):
            k = kern[layer, p, q]
            kt = k.T
            for u in range(2):
                a = ((p + u) * 3 + q) * LANES
                forward[a : a + LANES, u * LANES : (u + 1) * LANES] = k
                b = ((2 - p + u) * 3 + 2 - q) * LANES
                backward[b : b + LANES, u * LANES : (u + 1) * LANES] = kt


def windows(ref, row, s, left=0):
    out = []
    for t in range(4):
        for q in range(3):
            v = ref[pl.ds(row + t * s, s), left + q * s : left + q * s + T]
            out.append(v.reshape(s * T * 16, LANES))
    return jnp.concatenate(out, axis=1)


def stacked(ref, row, s, rows):
    return jnp.concatenate(
        [windows(ref, row + 2 * s * n, s) for n in range(rows // (2 * s))], axis=0
    )


def convolve(ref, weights, row, s, rows):
    both = jnp.dot(stacked(ref, row, s, rows), weights[...], preferred_element_type=F32)
    out = []
    m = T * 16
    for r in range(rows):
        n, u, e = r // (2 * s), (r // s) % 2, r % s
        at0 = (n * s + e) * m
        out.append(both[at0 : at0 + m, u * LANES : (u + 1) * LANES].reshape(T, 16, LANES))
    return out


def swap(low, n0, n1):
    return jnp.where(low, n0, pltpu.roll(n1, 4, 1)), jnp.where(low, pltpu.roll(n0, 4, 1), n1)


def low_half():
    return lax.broadcasted_iota(jnp.int32, (T // 2, 8, LANES), 1) < 4


def into_blocks(ref, c):
    low = low_half()
    n = [ref[CELL * c + e].astype(F32).reshape(T // 2, 8, LANES) for e in range(4)]
    lo = swap(low, n[0], n[1])
    hi = swap(low, n[2], n[3])
    both = [jnp.concatenate([lo[k], hi[k]], axis=1) for k in range(2)]
    return jnp.stack(both, axis=1).reshape(T, 16, LANES)


def out_of_blocks(ref, c, v):
    low = low_half()
    v = v.reshape(T // 2, 2, 16, LANES)
    for h in range(2):
        part = swap(low, v[:, 0, 8 * h : 8 * h + 8], v[:, 1, 8 * h : 8 * h + 8])
        for k in range(2):
            ref[CELL * c + 2 * h + k] = part[k].reshape(T * CELL, LANES).astype(ref.dtype)


def kernel(
    remote, f_hbm, g_hbm, kern, limit_ref, om_hbm, fg_hbm, res,
    fn, gn, f, a1, s1, a2, g2, g1, gf, w1, w1b, w2, w2b, rowm, colm, dw,
    full, got0, wxy, gxy, zbuf,
    local_sem, halo_send, halo_recv, ar_send, ar_recv,
):
    i, j, x, y, z, core = place()
    friends = [(lax.rem(i + dr + 16, 16), lax.rem(j + dc + 16, 16)) for dr, dc in SIDES]
    core_friend = at(x, y, z, 1 - core)
    z_friends = [at(x, y, flip(z, k), core) for k in range(1, 8)]
    xy = [(flip(x, k // 4), flip(y, k % 4)) for k in range(1, 16)]
    xy_friends = [at(a, b, z, core) for a, b in xy]
    if remote:
        barrier = pltpu.get_barrier_semaphore()
        everyone = friends + [core_friend] + z_friends + xy_friends
        for d in everyone:
            pl.semaphore_signal(barrier, inc=1, device_id=d, device_id_type=MESH)
    local = [
        pltpu.make_async_copy(f_hbm, fn, local_sem.at[0]),
        pltpu.make_async_copy(g_hbm, gn, local_sem.at[1]),
    ]
    for c in local:
        c.start()
    started = []

    def send(source, target, send_sem, recv_sem, device):
        c = pltpu.make_async_remote_copy(
            src_ref=source, dst_ref=target, send_sem=send_sem, recv_sem=recv_sem,
            device_id=device, device_id_type=MESH,
        )
        c.start()
        started.append(c)
        return c

    def exchange(n, ref, h):
        if not remote:
            return lambda: None
        src = {-1: pl.ds(h, h), 0: pl.ds(h, T), 1: pl.ds(T, h)}
        dst = {-1: pl.ds(h + T, h), 0: pl.ds(h, T), 1: pl.ds(0, h)}
        copies = [
            send(
                ref.at[src[dr], src[dc]], ref.at[dst[dr], dst[dc]],
                halo_send.at[n, m], halo_recv.at[n, m], friends[m],
            )
            for m, (dr, dc) in enumerate(SIDES)
        ]

        def finish():
            for c in copies:
                c.wait_recv()
            strips = [
                (i == 0, pl.ds(0, h), pl.ds(0, T + 2 * h)),
                (i == 15, pl.ds(T + h, h), pl.ds(0, T + 2 * h)),
                (j == 0, pl.ds(0, T + 2 * h), pl.ds(0, h)),
                (j == 15, pl.ds(0, T + 2 * h), pl.ds(T + h, h)),
            ]
            for edge, r, c in strips:

                @pl.when(edge)
                def _():
                    ref[r, c] = jnp.zeros((r.size, c.size, 16, LANES), BF16)

        return finish

    limit = limit_ref[0]
    sub = lax.broadcasted_iota(jnp.int32, (T, 16, LANES), 1)
    blk = lax.broadcasted_iota(jnp.int32, (T, 16, LANES), 0) * CELL
    rowm[...] = jnp.where(blk + sub // CELL + i * (T * CELL) < limit, 1.0, 0.0).astype(F32)
    colm[...] = jnp.where(blk + sub % CELL + j * (T * CELL) < limit, 1.0, 0.0).astype(F32)
    own1, own2 = pl.ds(ONE, T), pl.ds(TWO, T)

    def prepare_f(c, _):
        v = into_blocks(fn, c)
        f[c] = v.astype(BF16)
        a1[c + ONE, own1] = (elu(v) * (rowm[c] * colm[...])).astype(BF16)
        return 0

    def prepare_g(c, _):
        v = into_blocks(gn, c)
        g2[c + TWO, own2] = (v * (rowm[c] * colm[...])).astype(BF16)
        return 0

    local[0].wait()
    lax.fori_loop(0, T, prepare_f, 0)
    local[1].wait()
    lax.fori_loop(0, T, prepare_g, 0)
    if remote:
        pl.semaphore_wait(barrier, len(everyone))
    finish_a1 = exchange(0, a1, ONE)
    finish_g2 = exchange(1, g2, TWO)
    fill_weights(kern, w1, w1b, 0)
    fill_weights(kern, w2, w2b, 1)

    def conv1(k, _):
        for e, v in enumerate(convolve(a1, w1, k * R, ONE, R)):
            r = k * R + e
            v = v + f[r].astype(F32)
            s1[r] = v
            a2[r + TWO, own2] = (elu(v) * (rowm[r] * colm[...])).astype(BF16)
        return 0

    finish_a1()
    lax.fori_loop(0, T // R, conv1, 0)
    finish_a2 = exchange(2, a2, TWO)

    def contract(own, o, wide, s, layer, turned):
        def step(k, _):
            lhs = []
            for n in range(8 // (2 * s)):
                b = k * 8 + 2 * s * n
                gs = [
                    own[pl.ds(b + o + u * s, s), o : o + T].reshape(s * T * 16, LANES)
                    for u in range(2)
                ]
                lhs.append(jnp.concatenate(gs, axis=1))
            lhs = jnp.concatenate(lhs, axis=0)
            rhs = stacked(wide, k * 8, s, 8)
            part = lax.dot_general(lhs, rhs, (((0,), (0,)), ((), ())), preferred_element_type=F32)

            @pl.when(k == 0)
            def _():
                dw[...] = part

            @pl.when(k != 0)
            def _():
                dw[...] += part

            return 0

        lax.fori_loop(0, 2, step, 0)
        for p in range(3):
            for q in range(3):
                a, b = (p, q) if turned else (2 - p, 2 - q)
                lo = (a * 3 + b) * LANES
                hi = ((a + 1) * 3 + b) * LANES
                v = dw[:LANES, lo : lo + LANES] + dw[LANES:, hi : hi + LANES]
                v = (v.T if turned else v).reshape(2, 8, 8, LANES)
                for h in range(2):
                    n = (p * 3 + q) * 16 + 8 * h
                    full[layer, n // HALF, n % HALF : n % HALF + 8] = v[h]
        full[layer, :, HALF:] = jnp.zeros((2, PADDED - HALF, 8, LANES), F32)

    mine = x * 4 + y
    mine_at = pl.ds(mine * PIECE, PIECE)

    class Reduction:
        def __init__(self, layer):
            self.layer, self.slot, self.pending = layer, 0, []

        def send(self, source, target, device):
            n = self.slot
            self.slot += 1
            sems = ar_send.at[self.layer, n], ar_recv.at[self.layer, n]
            self.pending.append(send(source, target, *sems, device))

        def arrive(self):
            for c in self.pending:
                c.wait_recv()
            self.pending = []

        def core_out(self):
            n = self.layer
            if remote:
                self.send(full.at[n, 1 - core], got0.at[n], core_friend)

        def plane_out(self):
            n = self.layer
            if not remote:
                return
            self.arrive()
            v = full[n, core] + got0[n]
            full[n, core] = v
            wxy[n] = v.reshape(16, PIECE, 8, LANES).astype(WIRE)
            for k, (a, b) in enumerate(xy):
                self.send(wxy.at[n, a * 4 + b], gxy.at[n, k], xy_friends[k])

        def z_out(self):
            n = self.layer
            if not remote:
                return
            self.arrive()
            v = full[n, core, mine_at]
            for k in range(15):
                v = v + gxy[n, k].astype(F32)
            zbuf[n, z] = v.astype(WIRE)
            for d in z_friends:
                self.send(zbuf.at[n, z], zbuf.at[n, z], d)

        def plane_back(self):
            n = self.layer
            if not remote:
                return
            self.arrive()
            v = zbuf[n, 0].astype(F32)
            for k in range(1, 8):
                v = v + zbuf[n, k].astype(F32)
            res[n, core, mine_at] = (v / limit.astype(F32)).astype(WIRE)
            piece = res.at[n, core, mine_at]
            for d in xy_friends:
                self.send(piece, piece, d)

        def core_back(self):
            n = self.layer
            if not remote:
                res[n] = (full[n] / limit.astype(F32)).astype(WIRE)
                return
            self.arrive()
            self.send(res.at[n, core], res.at[n, core], core_friend)

    second, first = Reduction(1), Reduction(0)

    finish_g2()
    contract(a2, TWO, g2, TWO, 1, False)
    second.core_out()

    def back2(k, _):
        for e, v in enumerate(convolve(g2, w2b, k * R, TWO, R)):
            r = k * R + e
            m = rowm[r] * colm[...]
            v = g2[r + TWO, own2].astype(F32) + m * slope(s1[r]) * v
            gf[r] = v
            g1[r + ONE, own1] = v.astype(BF16)
        return 0

    lax.fori_loop(0, T // R // 2, back2, 0)
    second.plane_out()
    lax.fori_loop(T // R // 2, T // R, back2, 0)
    finish_g1 = exchange(3, g1, ONE)
    contract(g1, ONE, a1, ONE, 0, True)
    first.core_out()
    second.z_out()
    first.plane_out()

    def conv2(k, _):
        for e, v in enumerate(convolve(a2, w2, k * R, TWO, R)):
            r = k * R + e
            out_of_blocks(fn, r, rowm[r] * colm[...] * (s1[r] + v))
        return 0

    finish_a2()
    lax.fori_loop(0, T // R, conv2, 0)
    om = pltpu.make_async_copy(fn, om_hbm, local_sem.at[2])
    om.start()
    second.plane_back()

    def back1(k, _):
        for e, v in enumerate(convolve(g1, w1b, k * R, ONE, R)):
            r = k * R + e
            m = rowm[r] * colm[...]
            out_of_blocks(gn, r, gf[r] + m * slope(f[r].astype(F32)) * v)
        return 0

    finish_g1()
    lax.fori_loop(0, T // R // 2, back1, 0)
    first.z_out()
    lax.fori_loop(T // R // 2, T // R, back1, 0)
    fg = pltpu.make_async_copy(gn, fg_hbm, local_sem.at[3])
    fg.start()
    second.core_back()
    first.plane_back()
    second.arrive()
    first.core_back()
    om.wait()
    fg.wait()
    first.arrive()
    for c in started:
        c.wait_send()


R = 4


def call(remote, f, g, kernels, length):
    vm = pltpu.VMEM
    sems = pltpu.SemaphoreType.DMA
    tile = (T * CELL, T * CELL, LANES)

    def blocks(h, kind):
        return vm((T + 2 * h, T + 2 * h, 16, LANES), kind)

    return pl.pallas_call(
        functools.partial(kernel, remote),
        out_shape=(
            jax.ShapeDtypeStruct(tile, BF16),
            jax.ShapeDtypeStruct(tile, BF16),
            jax.ShapeDtypeStruct((2, 2, PADDED, 8, LANES), WIRE),
        ),
        in_specs=[
            pl.BlockSpec(memory_space=pl.ANY),
            pl.BlockSpec(memory_space=pl.ANY),
            pl.BlockSpec(memory_space=pltpu.VMEM),
            pl.BlockSpec(memory_space=pltpu.SMEM),
        ],
        out_specs=[
            pl.BlockSpec(memory_space=pl.ANY),
            pl.BlockSpec(memory_space=pl.ANY),
            pl.BlockSpec(memory_space=pltpu.VMEM),
        ],
        scratch_shapes=[
            vm(tile, BF16),
            vm(tile, BF16),
            blocks(0, BF16),
            blocks(ONE, BF16),
            blocks(0, F32),
            blocks(TWO, BF16),
            blocks(TWO, BF16),
            blocks(ONE, BF16),
            blocks(0, F32),
            vm((12 * LANES, 2 * LANES), BF16),
            vm((12 * LANES, 2 * LANES), BF16),
            vm((12 * LANES, 2 * LANES), BF16),
            vm((12 * LANES, 2 * LANES), BF16),
            vm((T, 16, LANES), F32),
            vm((T, 16, LANES), F32),
            vm((2 * LANES, 12 * LANES), F32),
            vm((2, 2, PADDED, 8, LANES), F32),
            vm((2, PADDED, 8, LANES), F32),
            vm((2, 16, PIECE, 8, LANES), WIRE),
            vm((2, 15, PIECE, 8, LANES), WIRE),
            vm((2, 8, PIECE, 8, LANES), WIRE),
            sems((4,)),
            sems((4, 8)),
            sems((4, 8)),
            sems((2, 39)),
            sems((2, 39)),
        ],
        compiler_params=pltpu.CompilerParams(
            collective_id=0 if remote else None, has_side_effects=True, vmem_limit_bytes=60 << 20
        ),
    )(f, g, kernels, length)


def body(features, kernels, length, cotangent):
    om, fg, kg = call(True, features, cotangent, kernels, length)
    kg = kg[:, :, :HALF].astype(F32).reshape(kernels.shape)
    return om, fg, kg


def solution(mesh):
    in_specs = (P("row", "col", None), P(), P(), P("row", "col", None))
    out_specs = (P("row", "col", None), P("row", "col", None), P())
    return jax.shard_map(body, mesh=mesh, in_specs=in_specs, out_specs=out_specs, check_vma=False)
```

profile of v0, /device:TPU:1, one launch (start us, length us, event | category | flops | bytes accessed | tf_op | source)
XLA Modules:
  0.0 62.7 jit_solution(2005432982816487973)
XLA Ops:
  1.3 56.1 %shard_map.67 = (bf16[64,64,128]{2,1,0:T(8,128)(2,1)}, bf16[64,64,128]{2,1,0:T(8,128)(2,1)}, bf16[2,2,80,8,128]{4,3,2,1,0:T(8,128)(2,1)}) custom-call(bf16[64,64,128]{2,1,0:T(8,128)(2,1)} %f_hbm.1, bf16[64,64,128]{2,1,0:T(8,128)(2,1)} %g_hbm.1, bf16[2,3,3,128,128]{4,3,2,1,0:T(8,128)(2,1)} %kern.1, s32[1]{0:T(128)S(6)} %copy.9.limit_ref), custom_call_target="tpu_custom_call" | custom-call | tf_op jit(solution)/shard_map/pallas_call | solution.py:404
  57.4 1.1 %slice.3 = bf16[2,2,72,8,128]{4,3,2,1,0:T(8,128)(2,1)S(1)} slice(bf16[2,2,80,8,128]{4,3,2,1,0:T(8,128)(2,1)} %get-tuple-element.8), slice={[0:2], [0:2], [0:72], [0:8], [0:128]} | slice | bytes 1179648 | tf_op jit(solution)/shard_map/slice | solution.py:458
  58.5 0.0 copy-start.1
  58.5 1.1 %convert.1 = f32[2,3,3,128,128]{4,3,2,1,0:T(8,128)} convert(bf16[2,3,3,128,128]{4,3,2,1,0:T(8,128)(2,1)S(1)} %bitcast.2) | non-fusion elementwise | flops 294912 | bytes 1769472 | tf_op jit(solution)/shard_map/reshape | solution.py:458
  59.7 0.5 copy-done.1
  60.2 0.0 copy-start
  60.2 1.0 %copy.10 = bf16[64,64,128]{2,1,0:T(8,128)(2,1)} copy(bf16[64,64,128]{2,1,0:T(8,128)(2,1)S(1)} %copy-done.1) | data formatting | bytes 2097152
  61.1 0.6 %copy-done = bf16[64,64,128]{2,1,0:T(8,128)(2,1)S(1)} copy-done((bf16[64,64,128]{2,1,0:T(8,128)(2,1)S(1)}, bf16[64,64,128]{2,1,0:T(8,128)(2,1)}, u32[]{:S(2)}) %copy-start) | copy-done | bytes 1048600
  61.8 1.0 %copy.11 = bf16[64,64,128]{2,1,0:T(8,128)(2,1)} copy(bf16[64,64,128]{2,1,0:T(8,128)(2,1)S(1)} %copy-done) | data formatting | bytes 2097152
Async XLA Ops:
  58.5 1.6 %copy-start.1 = (bf16[64,64,128]{2,1,0:T(8,128)(2,1)S(1)}, bf16[64,64,128]{2,1,0:T(8,128)(2,1)}, u32[]{:S(2)}) copy-start(bf16[64,64,128]{2,1,0:T(8,128)(2,1)} %get-tuple-element.12) | copy-start | bytes 3145732
  60.2 1.6 %copy-start = (bf16[64,64,128]{2,1,0:T(8,128)(2,1)S(1)}, bf16[64,64,128]{2,1,0:T(8,128)(2,1)}, u32[]{:S(2)}) copy-start(bf16[64,64,128]{2,1,0:T(8,128)(2,1)} %get-tuple-element.13) | copy-start | bytes 3145732
where the time goes:
time: 63 us; the launch traced here: 62.7 us
  Pallas kernels  56.1 us (89%)
  local copies, waits for them, and re-layouts  4.16 us (7%)
  between operations  1.3 us (2%)
  other arithmetic  1.14 us (2%)
    pallas_call x1, Pallas kernels, call(): pl.pallas_call(functools.partial(kernel, remote), out_shape=(jax.ShapeDty...  56.1 us
    unnamed x6, local copies, waits for them, and re-layouts  3.05 us

commit v1 on v0

--- a/solution.py
+++ b/solution.py
@@ -20,6 +20,7 @@
 PIECE = 5
 PADDED = 16 * PIECE
 WIRE = BF16
+HOPS = [(0, 1, 2, 1)[k // 4] + (0, 1, 2, 1)[k % 4] for k in range(1, 16)]
 
 
 def exp_low(values):
@@ -123,7 +124,7 @@
 
 def kernel(
     remote, f_hbm, g_hbm, kern, limit_ref, om_hbm, fg_hbm, res,
-    fn, gn, f, a1, s1, a2, g2, g1, gf, w1, w1b, w2, w2b, rowm, colm, dw,
+    fn, gn, f, a1, a1_rows, a1_cols, s1, a2, g2, g2_rows, g2_cols, g1, gf, w1, w1b, w2, w2b, rowm, colm, dw,
     full, got0, wxy, gxy, zbuf,
     local_sem, halo_send, halo_recv, ar_send, ar_recv,
 ):
@@ -185,6 +186,83 @@
 
         return finish
 
+    def strips(n, ref, h, rows, cols):
+        for ref_part in (cols.at[:, pl.ds(0, h)], cols.at[:, pl.ds(T + h, h)]):
+            ref_part[...] = jnp.zeros((2, h, h, 16, LANES), BF16)
+        copies = []
+        if remote:
+            src = {-1: pl.ds(h, h), 0: pl.ds(h, T), 1: pl.ds(T, h)}
+            dst = {-1: pl.ds(h + T, h), 0: pl.ds(h, T), 1: pl.ds(0, h)}
+            for m, (dr, dc) in enumerate(SIDES):
+                if dr:
+                    target = rows.at[(1 - dr) // 2, pl.ds(0, h), dst[dc]]
+                else:
+                    target = cols.at[(1 - dc) // 2, dst[0]]
+                copies.append(
+                    send(
+                        ref.at[src[dr], src[dc]], target,
+                        halo_send.at[n, m], halo_recv.at[n, m], friends[m],
+                    )
+                )
+
+        def finish():
+            for c in copies:
+                c.wait_recv()
+            for k, edge in enumerate((0, 15)):
+
+                @pl.when(i == edge)
+                def _():
+                    rows[k] = jnp.zeros((h, T + 2 * h, 16, LANES), BF16)
+
+                @pl.when(j == edge)
+                def _():
+                    rows[:, :, k * (T + h) : k * (T + h) + h] = jnp.zeros(
+                        (2, h, h, 16, LANES), BF16
+                    )
+                    cols[k] = jnp.zeros((T + 2 * h, h, 16, LANES), BF16)
+
+            for k in range(2):
+                lo = k * (T + h)
+                ref[h : T + h, lo : lo + h] = cols[k, h : T + h]
+                ref[lo : lo + h] = rows[k]
+
+        return finish
+
+    def borders(weights, h, rows, cols):
+        def product(parts, taps):
+            lhs = jnp.concatenate([v.reshape(h * T * 16, LANES) for v in parts], axis=1)
+            rhs = jnp.concatenate(
+                [weights[n * LANES : (n + 1) * LANES, :LANES] for n in taps], axis=0
+            )
+            return jnp.dot(lhs, rhs, preferred_element_type=F32)
+
+        out = []
+        for k in range(2):
+            v = product(
+                [rows[k, :, q * h : q * h + T] for q in range(3)],
+                [2 * k * 3 + q for q in range(3)],
+            )
+            out.append((pl.ds(k * (T - h), h), pl.ds(0, T), v.reshape(h, T, 16, LANES)))
+        for k in range(2):
+            v = product(
+                [cols[k, p * h : p * h + T] for p in range(3)],
+                [p * 3 + 2 * k for p in range(3)],
+            )
+            out.append((pl.ds(0, T), pl.ds(k * (T - h), h), v.reshape(T, h, 16, LANES)))
+        return out
+
+    def zero_border(ref, h):
+        ref[0:h] = jnp.zeros((h, T + 2 * h, 16, LANES), BF16)
+        ref[T + h :] = jnp.zeros((h, T + 2 * h, 16, LANES), BF16)
+        ref[:, 0:h] = jnp.zeros((T + 2 * h, h, 16, LANES), BF16)
+        ref[:, T + h :] = jnp.zeros((T + 2 * h, h, 16, LANES), BF16)
+
+    def live(r, c):
+        return rowm[r][:, None] * colm[c][None]
+
+    def shifted(d, n):
+        return pl.ds(d.start + n, d.size)
+
     limit = limit_ref[0]
     sub = lax.broadcasted_iota(jnp.int32, (T, 16, LANES), 1)
     blk = lax.broadcasted_iota(jnp.int32, (T, 16, LANES), 0) * CELL
@@ -203,14 +281,16 @@
         g2[c + TWO, own2] = (v * (rowm[c] * colm[...])).astype(BF16)
         return 0
 
+    zero_border(a1, ONE)
+    zero_border(g2, TWO)
     local[0].wait()
     lax.fori_loop(0, T, prepare_f, 0)
     local[1].wait()
     lax.fori_loop(0, T, prepare_g, 0)
     if remote:
         pl.semaphore_wait(barrier, len(everyone))
-    finish_a1 = exchange(0, a1, ONE)
-    finish_g2 = exchange(1, g2, TWO)
+    finish_a1 = strips(0, a1, ONE, a1_rows, a1_cols)
+    finish_g2 = strips(1, g2, TWO, g2_rows, g2_cols)
     fill_weights(kern, w1, w1b, 0)
     fill_weights(kern, w2, w2b, 1)
 
@@ -222,35 +302,27 @@
             a2[r + TWO, own2] = (elu(v) * (rowm[r] * colm[...])).astype(BF16)
         return 0
 
+    lax.fori_loop(0, T // R, conv1, 0)
     finish_a1()
-    lax.fori_loop(0, T // R, conv1, 0)
+    edges = borders(w1, ONE, a1_rows, a1_cols)
+    for r, c, v in edges:
+        s1[r, c] += v
+    for r, c, _ in edges:
+        a2[shifted(r, TWO), shifted(c, TWO)] = (elu(s1[r, c]) * live(r, c)).astype(BF16)
     finish_a2 = exchange(2, a2, TWO)
 
     def contract(own, o, wide, s, layer, turned):
-        def step(k, _):
-            lhs = []
-            for n in range(8 // (2 * s)):
-                b = k * 8 + 2 * s * n
-                gs = [
-                    own[pl.ds(b + o + u * s, s), o : o + T].reshape(s * T * 16, LANES)
-                    for u in range(2)
-                ]
-                lhs.append(jnp.concatenate(gs, axis=1))
-            lhs = jnp.concatenate(lhs, axis=0)
-            rhs = stacked(wide, k * 8, s, 8)
-            part = lax.dot_general(lhs, rhs, (((0,), (0,)), ((), ())), preferred_element_type=F32)
-
-            @pl.when(k == 0)
-            def _():
-                dw[...] = part
-
-            @pl.when(k != 0)
-            def _():
-                dw[...] += part
-
-            return 0
-
-        lax.fori_loop(0, 2, step, 0)
+        lhs = []
+        for n in range(T // (2 * s)):
+            b = 2 * s * n
+            gs = [
+                own[pl.ds(b + o + u * s, s), o : o + T].reshape(s * T * 16, LANES)
+                for u in range(2)
+            ]
+            lhs.append(jnp.concatenate(gs, axis=1))
+        lhs = jnp.concatenate(lhs, axis=0)
+        rhs = stacked(wide, 0, s, T)
+        dw[...] = lax.dot_general(lhs, rhs, (((0,), (0,)), ((), ())), preferred_element_type=F32)
         for p in range(3):
             for q in range(3):
                 a, b = (p, q) if turned else (2 - p, 2 - q)
@@ -321,20 +393,21 @@
             piece = res.at[n, core, mine_at]
             for d in xy_friends:
                 self.send(piece, piece, d)
+            self.coming, self.pending = self.pending, []
+            self.send(piece, piece, core_friend)
 
         def core_back(self):
             n = self.layer
             if not remote:
                 res[n] = (full[n] / limit.astype(F32)).astype(WIRE)
                 return
-            self.arrive()
-            self.send(res.at[n, core], res.at[n, core], core_friend)
+            for k in sorted(range(15), key=lambda k: HOPS[k]):
+                self.coming[k].wait_recv()
+                a, b = xy[k]
+                piece = res.at[n, core, pl.ds((a * 4 + b) * PIECE, PIECE)]
+                self.send(piece, piece, core_friend)
 
     second, first = Reduction(1), Reduction(0)
-
-    finish_g2()
-    contract(a2, TWO, g2, TWO, 1, False)
-    second.core_out()
 
     def back2(k, _):
         for e, v in enumerate(convolve(g2, w2b, k * R, TWO, R)):
@@ -345,14 +418,19 @@
             g1[r + ONE, own1] = v.astype(BF16)
         return 0
 
-    lax.fori_loop(0, T // R // 2, back2, 0)
-    second.plane_out()
-    lax.fori_loop(T // R // 2, T // R, back2, 0)
+    lax.fori_loop(0, T // R, back2, 0)
+    finish_g2()
+    edges = borders(w2b, TWO, g2_rows, g2_cols)
+    for r, c, v in edges:
+        gf[r, c] += live(r, c) * slope(s1[r, c]) * v
+    for r, c, _ in edges:
+        g1[shifted(r, ONE), shifted(c, ONE)] = gf[r, c].astype(BF16)
     finish_g1 = exchange(3, g1, ONE)
+    contract(a2, TWO, g2, TWO, 1, False)
+    second.core_out()
     contract(g1, ONE, a1, ONE, 0, True)
     first.core_out()
-    second.z_out()
-    first.plane_out()
+    second.plane_out()
 
     def conv2(k, _):
         for e, v in enumerate(convolve(a2, w2, k * R, TWO, R)):
@@ -361,10 +439,11 @@
         return 0
 
     finish_a2()
-    lax.fori_loop(0, T // R, conv2, 0)
+    lax.fori_loop(0, T // R // 2, conv2, 0)
+    first.plane_out()
+    lax.fori_loop(T // R // 2, T // R, conv2, 0)
     om = pltpu.make_async_copy(fn, om_hbm, local_sem.at[2])
     om.start()
-    second.plane_back()
 
     def back1(k, _):
         for e, v in enumerate(convolve(g1, w1b, k * R, ONE, R)):
@@ -375,22 +454,24 @@
 
     finish_g1()
     lax.fori_loop(0, T // R // 2, back1, 0)
-    first.z_out()
+    second.z_out()
     lax.fori_loop(T // R // 2, T // R, back1, 0)
     fg = pltpu.make_async_copy(gn, fg_hbm, local_sem.at[3])
     fg.start()
+    first.z_out()
+    second.plane_back()
+    first.plane_back()
     second.core_back()
-    first.plane_back()
-    second.arrive()
     first.core_back()
     om.wait()
     fg.wait()
+    second.arrive()
     first.arrive()
     for c in started:
         c.wait_send()
 
 
-R = 4
+R = 8
 
 
 def call(remote, f, g, kernels, length):
@@ -424,9 +505,13 @@
             vm(tile, BF16),
             blocks(0, BF16),
             blocks(ONE, BF16),
+            vm((2, ONE, T + 2 * ONE, 16, LANES), BF16),
+            vm((2, T + 2 * ONE, ONE, 16, LANES), BF16),
             blocks(0, F32),
             blocks(TWO, BF16),
             blocks(TWO, BF16),
+            vm((2, TWO, T + 2 * TWO, 16, LANES), BF16),
+            vm((2, T + 2 * TWO, TWO, 16, LANES), BF16),
             blocks(ONE, BF16),
             blocks(0, F32),
             vm((12 * LANES, 2 * LANES), BF16),
@@ -444,8 +529,8 @@
             sems((4,)),
             sems((4, 8)),
             sems((4, 8)),
-            sems((2, 39)),
-            sems((2, 39)),
+            sems((2, 54)),
+            sems((2, 54)),
         ],
         compiler_params=pltpu.CompilerParams(
             collective_id=0 if remote else None, has_side_effects=True, vmem_limit_bytes=60 << 20
@@ -453,10 +538,53 @@
     )(f, g, kernels, length)
 
 
+def place_kernel(om_in, fg_in, kg_in, om_out, fg_out, kg_out, a, b, k, wide, sems):
+    half = T * CELL // 2
+    moves = [(kg_in, k, None)]
+    for source, held, target in ((om_in, a, om_out), (fg_in, b, fg_out)):
+        for n in range(2):
+            d = pl.ds(n * half, half)
+            moves.append((source.at[d], held.at[d], target.at[d]))
+    ins = [
+        pltpu.make_async_copy(source, held, sems.at[0, n])
+        for n, (source, held, _) in enumerate(moves)
+    ]
+    for c in ins:
+        c.start()
+    outs = []
+    for n, (_, held, target) in enumerate(moves):
+        ins[n].wait()
+        if target is None:
+            wide[...] = k[:, :, :HALF].astype(F32)
+            held, target = wide, kg_out
+        c = pltpu.make_async_copy(held, target, sems.at[1, n])
+        c.start()
+        outs.append(c)
+    for c in outs:
+        c.wait()
+
+
 def body(features, kernels, length, cotangent):
     om, fg, kg = call(True, features, cotangent, kernels, length)
-    kg = kg[:, :, :HALF].astype(F32).reshape(kernels.shape)
-    return om, fg, kg
+    vm = pltpu.VMEM
+    om, fg, kg = pl.pallas_call(
+        place_kernel,
+        out_shape=(
+            jax.ShapeDtypeStruct(om.shape, om.dtype),
+            jax.ShapeDtypeStruct(fg.shape, fg.dtype),
+            jax.ShapeDtypeStruct((2, 2, HALF, 8, LANES), F32),
+        ),
+        in_specs=[pl.BlockSpec(memory_space=pl.ANY)] * 3,
+        out_specs=[pl.BlockSpec(memory_space=pl.ANY)] * 3,
+        scratch_shapes=[
+            vm(om.shape, om.dtype),
+            vm(fg.shape, fg.dtype),
+            vm(kg.shape, kg.dtype),
+            vm((2, 2, HALF, 8, LANES), F32),
+            pltpu.SemaphoreType.DMA((2, 5)),
+        ],
+    )(om, fg, kg)
+    return om, fg, kg.reshape(kernels.shape)
 
 
 def solution(mesh):

time: 63 us -> 58.6 us (0.930)
  local copies, waits for them, and re-layouts: 4.16 us -> 0 us
  other arithmetic: 1.14 us -> 0 us
  Pallas kernels: 56.1 us -> 56.9 us
    unnamed x6 -> x0, local copies, waits for them, and re-layouts: 3.05 us -> none
    pallas_call x0 -> x1, Pallas kernels: none -> 2.95 us  [body(): pl.pallas_call(place_kernel, out_shape=(jax.ShapeDtypeStruct(om.shape, om...]
    pallas_call x1, Pallas kernels: 56.1 us -> 54 us  [call(): pl.pallas_call(functools.partial(kernel, remote), out_shape=(jax.ShapeDty...]
    reshape x1 -> x0, other arithmetic: 1.14 us -> none  [body(): kg = kg[:, :, :HALF].astype(F32).reshape(kernels.shape)]
    slice x1 -> x0, local copies, waits for them, and re-layouts: 1.11 us -> none  [body(): kg = kg[:, :, :HALF].astype(F32).reshape(kernels.shape)]
where the time goes in v1:
time: 58.6 us; the launch traced here: 58.4 us
  Pallas kernels  56.9 us (97%)
  between operations  1.45 us (2%)
    pallas_call x1, Pallas kernels, call(): pl.pallas_call(functools.partial(kernel, remote), out_shape=(jax.ShapeDty...  54 us
    pallas_call x1, Pallas kernels, body(): pl.pallas_call(place_kernel, out_shape=(jax.ShapeDtypeStruct(om.shape, om...  2.95 us

profile of v1, /device:TPU:1, one launch (start us, length us, event | category | flops | bytes accessed | tf_op | source)
XLA Modules:
  0.0 58.4 jit_solution(14876745961102912325)
XLA Ops:
  1.3 54.0 %shard_map.67 = (bf16[64,64,128]{2,1,0:T(8,128)(2,1)}, bf16[64,64,128]{2,1,0:T(8,128)(2,1)}, bf16[2,2,80,8,128]{4,3,2,1,0:T(8,128)(2,1)}) custom-call(bf16[64,64,128]{2,1,0:T(8,128)(2,1)} %f_hbm.1, bf16[64,64,128]{2,1,0:T(8,128)(2,1)} %g_hbm.1, bf16[2,3,3,128,128]{4,3,2,1,0:T(8,128)(2,1)} %kern.1, s32[1]{0:T(128)S(6)} %copy.7.limit_ref), custom_call_target="tpu_custom_call" | custom-call | tf_op jit(solution)/shard_map/pallas_call | solution.py:485
  55.3 3.0 %shard_map.68 = (bf16[64,64,128]{2,1,0:T(8,128)(2,1)}, bf16[64,64,128]{2,1,0:T(8,128)(2,1)}, f32[2,2,72,8,128]{4,3,2,1,0:T(8,128)}) custom-call(bf16[64,64,128]{2,1,0:T(8,128)(2,1)} %get-tuple-element.9.om_in, bf16[64,64,128]{2,1,0:T(8,128)(2,1)} %get-tuple-element.10.fg_in, bf16[2,2,80,8,128]{4,3,2,1,0:T(8,128)(2,1)} %get-tuple-element.11.kg_in), custom_call_target="tpu_custom_call" | custom-call | tf_op jit(solution)/shard_map/pallas_call | solution.py:570

commit v2 on v1

--- a/solution.py
+++ b/solution.py
@@ -129,6 +129,9 @@
     local_sem, halo_send, halo_recv, ar_send, ar_recv,
 ):
     i, j, x, y, z, core = place()
+    def inside(dr, dc):
+        return (i + dr >= 0) & (i + dr < 16) & (j + dc >= 0) & (j + dc < 16)
+
     friends = [(lax.rem(i + dr + 16, 16), lax.rem(j + dc + 16, 16)) for dr, dc in SIDES]
     core_friend = at(x, y, z, 1 - core)
     z_friends = [at(x, y, flip(z, k), core) for k in range(1, 8)]
@@ -147,13 +150,16 @@
         c.start()
     started = []
 
-    def send(source, target, send_sem, recv_sem, device):
+    def send(source, target, send_sem, recv_sem, device, go=None):
         c = pltpu.make_async_remote_copy(
             src_ref=source, dst_ref=target, send_sem=send_sem, recv_sem=recv_sem,
             device_id=device, device_id_type=MESH,
         )
-        c.start()
-        started.append(c)
+        if go is None:
+            c.start()
+        else:
+            pl.when(go)(c.start)
+        started.append((c, go))
         return c
 
     def exchange(n, ref, h):
@@ -164,14 +170,14 @@
         copies = [
             send(
                 ref.at[src[dr], src[dc]], ref.at[dst[dr], dst[dc]],
-                halo_send.at[n, m], halo_recv.at[n, m], friends[m],
+                halo_send.at[n, m], halo_recv.at[n, m], friends[m], inside(dr, dc),
             )
             for m, (dr, dc) in enumerate(SIDES)
         ]
 
         def finish():
-            for c in copies:
-                c.wait_recv()
+            for c, (dr, dc) in zip(copies, SIDES):
+                pl.when(inside(-dr, -dc))(c.wait_recv)
             strips = [
                 (i == 0, pl.ds(0, h), pl.ds(0, T + 2 * h)),
                 (i == 15, pl.ds(T + h, h), pl.ds(0, T + 2 * h)),
@@ -201,13 +207,13 @@
                 copies.append(
                     send(
                         ref.at[src[dr], src[dc]], target,
-                        halo_send.at[n, m], halo_recv.at[n, m], friends[m],
+                        halo_send.at[n, m], halo_recv.at[n, m], friends[m], inside(dr, dc),
                     )
                 )
 
         def finish():
-            for c in copies:
-                c.wait_recv()
+            for c, (dr, dc) in zip(copies, SIDES):
+                pl.when(inside(-dr, -dc))(c.wait_recv)
             for k, edge in enumerate((0, 15)):
 
                 @pl.when(i == edge)
@@ -309,7 +315,6 @@
         s1[r, c] += v
     for r, c, _ in edges:
         a2[shifted(r, TWO), shifted(c, TWO)] = (elu(s1[r, c]) * live(r, c)).astype(BF16)
-    finish_a2 = exchange(2, a2, TWO)
 
     def contract(own, o, wide, s, layer, turned):
         lhs = []
@@ -438,13 +443,6 @@
             out_of_blocks(fn, r, rowm[r] * colm[...] * (s1[r] + v))
         return 0
 
-    finish_a2()
-    lax.fori_loop(0, T // R // 2, conv2, 0)
-    first.plane_out()
-    lax.fori_loop(T // R // 2, T // R, conv2, 0)
-    om = pltpu.make_async_copy(fn, om_hbm, local_sem.at[2])
-    om.start()
-
     def back1(k, _):
         for e, v in enumerate(convolve(g1, w1b, k * R, ONE, R)):
             r = k * R + e
@@ -452,23 +450,31 @@
             out_of_blocks(gn, r, gf[r] + m * slope(f[r].astype(F32)) * v)
         return 0
 
+    first.plane_out()
+    finish_a2 = exchange(2, a2, TWO)
+    second.z_out()
+    first.z_out()
     finish_g1()
-    lax.fori_loop(0, T // R // 2, back1, 0)
-    second.z_out()
-    lax.fori_loop(T // R // 2, T // R, back1, 0)
+    lax.fori_loop(0, T // R, back1, 0)
     fg = pltpu.make_async_copy(gn, fg_hbm, local_sem.at[3])
     fg.start()
-    first.z_out()
     second.plane_back()
     first.plane_back()
+    finish_a2()
+    lax.fori_loop(0, T // R, conv2, 0)
+    om = pltpu.make_async_copy(fn, om_hbm, local_sem.at[2])
+    om.start()
     second.core_back()
     first.core_back()
     om.wait()
     fg.wait()
     second.arrive()
     first.arrive()
-    for c in started:
-        c.wait_send()
+    for c, go in started:
+        if go is None:
+            c.wait_send()
+        else:
+            pl.when(go)(c.wait_send)
 
 
 R = 8
@@ -490,8 +496,8 @@
             jax.ShapeDtypeStruct((2, 2, PADDED, 8, LANES), WIRE),
         ),
         in_specs=[
-            pl.BlockSpec(memory_space=pl.ANY),
-            pl.BlockSpec(memory_space=pl.ANY),
+            pl.BlockSpec(memory_space=pltpu.HBM),
+            pl.BlockSpec(memory_space=pltpu.HBM),
             pl.BlockSpec(memory_space=pltpu.VMEM),
             pl.BlockSpec(memory_space=pltpu.SMEM),
         ],
@@ -533,35 +539,26 @@
             sems((2, 54)),
         ],
         compiler_params=pltpu.CompilerParams(
-            collective_id=0 if remote else None, has_side_effects=True, vmem_limit_bytes=60 << 20
+            collective_id=0 if remote else None, has_side_effects=True, vmem_limit_bytes=50 << 20
         ),
     )(f, g, kernels, length)
 
 
-def place_kernel(om_in, fg_in, kg_in, om_out, fg_out, kg_out, a, b, k, wide, sems):
-    half = T * CELL // 2
-    moves = [(kg_in, k, None)]
-    for source, held, target in ((om_in, a, om_out), (fg_in, b, fg_out)):
-        for n in range(2):
-            d = pl.ds(n * half, half)
-            moves.append((source.at[d], held.at[d], target.at[d]))
-    ins = [
-        pltpu.make_async_copy(source, held, sems.at[0, n])
-        for n, (source, held, _) in enumerate(moves)
+def place_kernel(om_in, fg_in, kg_in, om_out, fg_out, kg_out, k, wide, sems):
+    moves = [(kg_in, k), (om_in, om_out), (fg_in, fg_out)]
+    copies = [
+        pltpu.make_async_copy(source, target, sems.at[n])
+        for n, (source, target) in enumerate(moves)
     ]
-    for c in ins:
+    for c in copies:
         c.start()
-    outs = []
-    for n, (_, held, target) in enumerate(moves):
-        ins[n].wait()
-        if target is None:
-            wide[...] = k[:, :, :HALF].astype(F32)
-            held, target = wide, kg_out
-        c = pltpu.make_async_copy(held, target, sems.at[1, n])
-        c.start()
-        outs.append(c)
-    for c in outs:
+    copies[0].wait()
+    wide[...] = k[:, :, :HALF].astype(F32)
+    last = pltpu.make_async_copy(wide, kg_out, sems.at[3])
+    last.start()
+    for c in copies[1:]:
         c.wait()
+    last.wait()
 
 
 def body(features, kernels, length, cotangent):
@@ -577,12 +574,11 @@
         in_specs=[pl.BlockSpec(memory_space=pl.ANY)] * 3,
         out_specs=[pl.BlockSpec(memory_space=pl.ANY)] * 3,
         scratch_shapes=[
-            vm(om.shape, om.dtype),
-            vm(fg.shape, fg.dtype),
             vm(kg.shape, kg.dtype),
             vm((2, 2, HALF, 8, LANES), F32),
-            pltpu.SemaphoreType.DMA((2, 5)),
+            pltpu.SemaphoreType.DMA((4,)),
         ],
+        compiler_params=pltpu.CompilerParams(vmem_limit_bytes=8 << 20),
     )(om, fg, kg)
     return om, fg, kg.reshape(kernels.shape)
 

time: 58.6 us -> 54.4 us (0.928)
  Pallas kernels: 56.9 us -> 51.9 us
  local copies, waits for them, and re-layouts: 0 us -> 1.06 us
    pallas_call x1, Pallas kernels: 54 us -> 49.9 us  [call(): pl.pallas_call(functools.partial(kernel, remote), out_shape=(jax.ShapeDty...]
    unnamed x0 -> x2, local copies, waits for them, and re-layouts: none -> 1.06 us
    pallas_call x1, Pallas kernels: 2.95 us -> 1.94 us  [body(): pl.pallas_call(place_kernel, out_shape=(jax.ShapeDtypeStruct(om.shape, om...]
where the time goes in v2:
time: 54.4 us; the launch traced here: 54.2 us
  Pallas kernels  51.9 us (95%)
  between operations  1.29 us (2%)
  local copies, waits for them, and re-layouts  1.06 us (2%)
    pallas_call x1, Pallas kernels, call(): pl.pallas_call(functools.partial(kernel, remote), out_shape=(jax.ShapeDty...  49.9 us
    pallas_call x1, Pallas kernels, body(): pl.pallas_call(place_kernel, out_shape=(jax.ShapeDtypeStruct(om.shape, om...  1.94 us

profile of v2, /device:TPU:1, one launch (start us, length us, event | category | flops | bytes accessed | tf_op | source)
XLA Modules:
  0.0 54.2 jit_solution(17965823846575136594)
XLA Ops:
  1.3 0.0 copy-start
  1.3 1.1 %copy-done = bf16[2,3,3,128,128]{4,3,2,1,0:T(8,128)(2,1)S(1)} copy-done((bf16[2,3,3,128,128]{4,3,2,1,0:T(8,128)(2,1)S(1)}, bf16[2,3,3,128,128]{4,3,2,1,0:T(8,128)(2,1)}, u32[]{:S(2)}) %copy-start) | copy-done | bytes 589848
  2.3 49.9 %shard_map.67 = (bf16[64,64,128]{2,1,0:T(8,128)(2,1)S(1)}, bf16[64,64,128]{2,1,0:T(8,128)(2,1)S(1)}, bf16[2,2,80,8,128]{4,3,2,1,0:T(8,128)(2,1)S(1)}) custom-call(bf16[64,64,128]{2,1,0:T(8,128)(2,1)} %f_hbm.1, bf16[64,64,128]{2,1,0:T(8,128)(2,1)} %g_hbm.1, bf16[2,3,3,128,128]{4,3,2,1,0:T(8,128)(2,1)S(1)} %copy-done, s32[1]{0:T(128)S(6)} %copy.7.limit_ref), custom_call_target="tpu_custom_call" | custom-call | tf_op jit(solution)/shard_map/pallas_call | solution.py:491
  52.3 1.9 %shard_map.68 = (bf16[64,64,128]{2,1,0:T(8,128)(2,1)}, bf16[64,64,128]{2,1,0:T(8,128)(2,1)}, f32[2,2,72,8,128]{4,3,2,1,0:T(8,128)}) custom-call(bf16[64,64,128]{2,1,0:T(8,128)(2,1)S(1)} %get-tuple-element.9.om_in, bf16[64,64,128]{2,1,0:T(8,128)(2,1)S(1)} %get-tuple-element.10.fg_in, bf16[2,2,80,8,128]{4,3,2,1,0:T(8,128)(2,1)S(1)} %get-tuple-element.11.kg_in), custom_call_target="tpu_custom_call" | custom-call | tf_op jit(solution)/shard_map/pallas_call | solution.py:567
Async XLA Ops:
  1.3 1.1 %copy-start = (bf16[2,3,3,128,128]{4,3,2,1,0:T(8,128)(2,1)S(1)}, bf16[2,3,3,128,128]{4,3,2,1,0:T(8,128)(2,1)}, u32[]{:S(2)}) copy-start(bf16[2,3,3,128,128]{4,3,2,1,0:T(8,128)(2,1)} %kern.1) | copy-start | bytes 1769476

commit v3 on v2

--- a/solution.py
+++ b/solution.py
@@ -21,6 +21,7 @@
 PADDED = 16 * PIECE
 WIRE = BF16
 HOPS = [(0, 1, 2, 1)[k // 4] + (0, 1, 2, 1)[k % 4] for k in range(1, 16)]
+FAR_FIRST = sorted(range(15), key=lambda k: -HOPS[k])
 
 
 def exp_low(values):
@@ -291,11 +292,11 @@
     zero_border(g2, TWO)
     local[0].wait()
     lax.fori_loop(0, T, prepare_f, 0)
-    local[1].wait()
-    lax.fori_loop(0, T, prepare_g, 0)
     if remote:
         pl.semaphore_wait(barrier, len(everyone))
     finish_a1 = strips(0, a1, ONE, a1_rows, a1_cols)
+    local[1].wait()
+    lax.fori_loop(0, T, prepare_g, 0)
     finish_g2 = strips(1, g2, TWO, g2_rows, g2_cols)
     fill_weights(kern, w1, w1b, 0)
     fill_weights(kern, w2, w2b, 1)
@@ -371,7 +372,8 @@
             v = full[n, core] + got0[n]
             full[n, core] = v
             wxy[n] = v.reshape(16, PIECE, 8, LANES).astype(WIRE)
-            for k, (a, b) in enumerate(xy):
+            for k in FAR_FIRST:
+                a, b = xy[k]
                 self.send(wxy.at[n, a * 4 + b], gxy.at[n, k], xy_friends[k])
 
         def z_out(self):
@@ -383,8 +385,8 @@
             for k in range(15):
                 v = v + gxy[n, k].astype(F32)
             zbuf[n, z] = v.astype(WIRE)
-            for d in z_friends:
-                self.send(zbuf.at[n, z], zbuf.at[n, z], d)
+            for k in (4, 5, 3, 7, 6, 2, 1):
+                self.send(zbuf.at[n, z], zbuf.at[n, z], z_friends[k - 1])
 
         def plane_back(self):
             n = self.layer
@@ -396,9 +398,9 @@
                 v = v + zbuf[n, k].astype(F32)
             res[n, core, mine_at] = (v / limit.astype(F32)).astype(WIRE)
             piece = res.at[n, core, mine_at]
-            for d in xy_friends:
-                self.send(piece, piece, d)
-            self.coming, self.pending = self.pending, []
+            for k in FAR_FIRST:
+                self.send(piece, piece, xy_friends[k])
+            self.coming, self.pending = dict(zip(FAR_FIRST, self.pending)), []
             self.send(piece, piece, core_friend)
 
         def core_back(self):

time: 54.4 us -> 52.8 us (0.971)
  Pallas kernels: 51.9 us -> 50.3 us
    pallas_call x1, Pallas kernels: 49.9 us -> 48.4 us  [call(): pl.pallas_call(functools.partial(kernel, remote), out_shape=(jax.ShapeDty...]
where the time goes in v3:
time: 52.8 us; the launch traced here: 52.6 us
  Pallas kernels  50.3 us (95%)
  between operations  1.29 us (2%)
  local copies, waits for them, and re-layouts  1.06 us (2%)
    pallas_call x1, Pallas kernels, call(): pl.pallas_call(functools.partial(kernel, remote), out_shape=(jax.ShapeDty...  48.4 us
    pallas_call x1, Pallas kernels, body(): pl.pallas_call(place_kernel, out_shape=(jax.ShapeDtypeStruct(om.shape, om...  1.94 us
    unnamed x2, local copies, waits for them, and re-layouts  1.06 us

profile of v3, /device:TPU:1, one launch (start us, length us, event | category | flops | bytes accessed | tf_op | source)
XLA Modules:
  0.0 52.6 jit_solution(12477107846772697257)
XLA Ops:
  1.3 0.0 copy-start
  1.3 1.1 %copy-done = bf16[2,3,3,128,128]{4,3,2,1,0:T(8,128)(2,1)S(1)} copy-done((bf16[2,3,3,128,128]{4,3,2,1,0:T(8,128)(2,1)S(1)}, bf16[2,3,3,128,128]{4,3,2,1,0:T(8,128)(2,1)}, u32[]{:S(2)}) %copy-start) | copy-done | bytes 589848
  2.3 48.4 %shard_map.67 = (bf16[64,64,128]{2,1,0:T(8,128)(2,1)S(1)}, bf16[64,64,128]{2,1,0:T(8,128)(2,1)S(1)}, bf16[2,2,80,8,128]{4,3,2,1,0:T(8,128)(2,1)S(1)}) custom-call(bf16[64,64,128]{2,1,0:T(8,128)(2,1)} %f_hbm.1, bf16[64,64,128]{2,1,0:T(8,128)(2,1)} %g_hbm.1, bf16[2,3,3,128,128]{4,3,2,1,0:T(8,128)(2,1)S(1)} %copy-done, s32[1]{0:T(128)S(6)} %copy.7.limit_ref), custom_call_target="tpu_custom_call" | custom-call | tf_op jit(solution)/shard_map/pallas_call | solution.py:493
  50.7 1.9 %shard_map.68 = (bf16[64,64,128]{2,1,0:T(8,128)(2,1)}, bf16[64,64,128]{2,1,0:T(8,128)(2,1)}, f32[2,2,72,8,128]{4,3,2,1,0:T(8,128)}) custom-call(bf16[64,64,128]{2,1,0:T(8,128)(2,1)S(1)} %get-tuple-element.9.om_in, bf16[64,64,128]{2,1,0:T(8,128)(2,1)S(1)} %get-tuple-element.10.fg_in, bf16[2,2,80,8,128]{4,3,2,1,0:T(8,128)(2,1)S(1)} %get-tuple-element.11.kg_in), custom_call_target="tpu_custom_call" | custom-call | tf_op jit(solution)/shard_map/pallas_call | solution.py:569
Async XLA Ops:
  1.3 1.1 %copy-start = (bf16[2,3,3,128,128]{4,3,2,1,0:T(8,128)(2,1)S(1)}, bf16[2,3,3,128,128]{4,3,2,1,0:T(8,128)(2,1)}, u32[]{:S(2)}) copy-start(bf16[2,3,3,128,128]{4,3,2,1,0:T(8,128)(2,1)} %kern.1) | copy-start | bytes 1769476

commit v4 on v3

--- a/solution.py
+++ b/solution.py
@@ -15,7 +15,8 @@
 ONE, TWO = FIRST_SPACING // CELL, SECOND_SPACING // CELL
 T = 16
 LANES = 128
-SIDES = [(r, c) for r in (-1, 0, 1) for c in (-1, 0, 1) if (r, c) != (0, 0)]
+CORNERS = [(-1, -1), (-1, 1), (1, -1), (1, 1)]
+SIDES = CORNERS + [(0, -1), (0, 1), (-1, 0), (1, 0)]
 HALF = 72
 PIECE = 5
 PADDED = 16 * PIECE

time: 52.8 us -> 52.6 us (level)
  no operation moved by 1% of the time
where the time goes in v4:
time: 52.6 us; the launch traced here: 52.4 us
  Pallas kernels  50.1 us (95%)
  between operations  1.29 us (2%)
  local copies, waits for them, and re-layouts  1.06 us (2%)
    pallas_call x1, Pallas kernels, call(): pl.pallas_call(functools.partial(kernel, remote), out_shape=(jax.ShapeDty...  48.1 us
    pallas_call x1, Pallas kernels, body(): pl.pallas_call(place_kernel, out_shape=(jax.ShapeDtypeStruct(om.shape, om...  1.94 us
    unnamed x2, local copies, waits for them, and re-layouts  1.06 us

profile of v4, /device:TPU:1, one launch (start us, length us, event | category | flops | bytes accessed | tf_op | source)
XLA Modules:
  0.0 52.4 jit_solution(3058373232757528148)
XLA Ops:
  1.3 0.0 copy-start
  1.3 1.1 %copy-done = bf16[2,3,3,128,128]{4,3,2,1,0:T(8,128)(2,1)S(1)} copy-done((bf16[2,3,3,128,128]{4,3,2,1,0:T(8,128)(2,1)S(1)}, bf16[2,3,3,128,128]{4,3,2,1,0:T(8,128)(2,1)}, u32[]{:S(2)}) %copy-start) | copy-done | bytes 589848
  2.3 48.1 %shard_map.67 = (bf16[64,64,128]{2,1,0:T(8,128)(2,1)S(1)}, bf16[64,64,128]{2,1,0:T(8,128)(2,1)S(1)}, bf16[2,2,80,8,128]{4,3,2,1,0:T(8,128)(2,1)S(1)}) custom-call(bf16[64,64,128]{2,1,0:T(8,128)(2,1)} %f_hbm.1, bf16[64,64,128]{2,1,0:T(8,128)(2,1)} %g_hbm.1, bf16[2,3,3,128,128]{4,3,2,1,0:T(8,128)(2,1)S(1)} %copy-done, s32[1]{0:T(128)S(6)} %copy.7.limit_ref), custom_call_target="tpu_custom_call" | custom-call | tf_op jit(solution)/shard_map/pallas_call | solution.py:494
  50.5 1.9 %shard_map.68 = (bf16[64,64,128]{2,1,0:T(8,128)(2,1)}, bf16[64,64,128]{2,1,0:T(8,128)(2,1)}, f32[2,2,72,8,128]{4,3,2,1,0:T(8,128)}) custom-call(bf16[64,64,128]{2,1,0:T(8,128)(2,1)S(1)} %get-tuple-element.9.om_in, bf16[64,64,128]{2,1,0:T(8,128)(2,1)S(1)} %get-tuple-element.10.fg_in, bf16[2,2,80,8,128]{4,3,2,1,0:T(8,128)(2,1)S(1)} %get-tuple-element.11.kg_in), custom_call_target="tpu_custom_call" | custom-call | tf_op jit(solution)/shard_map/pallas_call | solution.py:570
Async XLA Ops:
  1.3 1.1 %copy-start = (bf16[2,3,3,128,128]{4,3,2,1,0:T(8,128)(2,1)S(1)}, bf16[2,3,3,128,128]{4,3,2,1,0:T(8,128)(2,1)}, u32[]{:S(2)}) copy-start(bf16[2,3,3,128,128]{4,3,2,1,0:T(8,128)(2,1)} %kern.1) | copy-start | bytes 1769476
